TPU v7x, 32 devices: a whole 2x2x4 slice. The times are simulated.
32 devices in a mesh: tm: 2 (over y), rows: 16 (over z, x, core).
Axes of the slice: x: 2, y: 2, z: 4, core: 2. Of those that a mesh axis runs over, the one named last changes fastest.
Arguments:
- frames_in: bfloat16 [8, 32, 96, 832], P('tm', 'rows'), may hold values from -6 to 6
- gain_first: float32 [96], replicated, may hold values from 0.1 to 1.9
- kernel_first: bfloat16 [3, 3, 3, 96, 96], replicated, may hold values from -0.125 to 0.125
- bias_first: float32 [96], replicated, may hold values from -3 to 3
- gain_second: float32 [96], replicated, may hold values from 0.1 to 1.9
- kernel_second: bfloat16 [3, 3, 3, 96, 96], replicated, may hold values from -0.125 to 0.125
- bias_second: float32 [96], replicated, may hold values from -3 to 3
Outputs:
- frames_out: bfloat16 [8, 32, 96, 832], P('tm', 'rows')
All inputs are finite; a program needn't handle non-finite values.
Results may differ from a plain program's by a relative error of at most 0.008.
Values may be sent and summed in bfloat16 or wider, within the bound.
A program may use at most 128 MiB of HBM per device.

v0:
```python
import jax
import jax.numpy as jnp
from jax import lax
from jax.sharding import PartitionSpec as P


def shifted(block, axis, distance):
    devices = range(lax.axis_size(axis))
    route = [(i - distance, i) for i in devices if i - distance in devices]
    return lax.ppermute(block, axis, route)


def padded(value, sides, width):
    for axis, dim in sides:
        size, length = (lax.axis_size(axis), value.shape[dim])
        up = [(i, (i + 1) % size) for i in range(size - 1)]
        down = [(j, i) for i, j in up]
        last = lax.slice_in_dim(value, length - width, length, axis=dim)
        initial = lax.slice_in_dim(value, 0, width, axis=dim)
        before = lax.ppermute(last, axis, up)
        after = lax.ppermute(initial, axis, down)
        value = jnp.concatenate([before, value, after], axis=dim)
    return value


def norm_silu(values, gain):
    wide = values.astype(jnp.float32)
    mean_square = jnp.mean(wide * wide, axis=-2, keepdims=True)
    scaled = wide * lax.rsqrt(mean_square + 1e-06) * gain[:, None]
    return jax.nn.silu(scaled).astype(jnp.bfloat16)


def extend(active, depth_frames, depth_rows):
    earlier = shifted(active[-depth_frames:], "tm", 1)
    joined = jnp.concatenate([earlier, active], axis=0)
    return padded(joined, (("rows", 1),), depth_rows)


def convolve(extended, kernel, bias):
    result = lax.conv_general_dilated(
        extended[None],
        kernel,
        window_strides=(1, 1, 1),
        padding=((0, 0), (0, 0), (1, 1)),
        dimension_numbers=("NDHCW", "DHWOI", "NDHCW"),
        preferred_element_type=jnp.float32,
    )[0]
    return result + bias[:, None]


def on_device(
    frames_in, gain_first, kernel_first, bias_first, gain_second, kernel_second, bias_second
):
    act_first = norm_silu(frames_in, gain_first)
    extended = extend(act_first, 2, 1)
    hidden = convolve(extended, kernel_first, bias_first).astype(jnp.bfloat16)
    act_second = norm_silu(hidden, gain_second)
    extended_second = extend(act_second, 2, 1)
    result = convolve(extended_second, kernel_second, bias_second)
    return (result + frames_in.astype(jnp.float32)).astype(jnp.bfloat16)


def solution(mesh):
    return jax.shard_map(
        on_device,
        mesh=mesh,
        in_specs=(P("tm", "rows", None, None), P(), P(), P(), P(), P(), P()),
        out_specs=P("tm", "rows", None, None),
        check_vma=False,
    )
```

profile of v0, /device:TPU:6, one launch (start us, length us, event | category | flops | bytes accessed | tf_op | source)
XLA Modules:
  0.0 199.5 jit_solution(2267612109716827066)
XLA Ops:
  0.0 0.0 copy-start
  0.0 1.7 fusion.24
  1.8 2.3 %fusion.31 = bf16[4,2,96,832]{3,2,1,0:T(8,128)(2,1)S(1)} fusion(bf16[4,2,96,832]{3,2,1,0:T(8,128)(2,1)} %param.7, f32[96]{0:T(128)} %param.8, f32[4,2,832]{2,1,0:T(2,128)S(1)} %add_rsqrt_fusion.1), kind=kLoop, calls=%fused_computation.37 | loop fusion | flops 5111808 | bytes 2582912 | tf_op jit(solution)/shard_map/convert_element_type | solution.py:30
  4.1 0.1 slice.28
  4.1 1.3 collective-permute-start
  5.4 17.8 %collective-permute-done = bf16[2,2,96,832]{3,2,1,0:T(8,128)(2,1)S(1)} collective-permute-done((bf16[2,2,96,832]{3,2,1,0:T(8,128)(2,1)S(1)}, bf16[2,2,96,832]{3,2,1,0:T(8,128)(2,1)S(1)}, u32[]{:S(2)}, u32[]{:S(2)}) %collective-permute-start) | collective-permute-done | bytes 639008 | tf_op jit(solution)/shard_map/ppermute | solution.py:10
  23.2 0.3 fusion.45
  23.4 1.9 collective-permute-start.1
  25.4 3.6 %collective-permute-start.2 = (bf16[6,1,96,832]{3,2,1,0:T(8,128)(2,1)S(1)}, bf16[6,1,96,832]{3,2,1,0:T(8,128)(2,1)S(1)}, u32[]{:S(2)}, u32[]{:S(2)}) collective-permute-start(bf16[6,1,96,832]{3,2,1,0:T(8,128)(2,1)S(1)} %get-tuple-element.8), channel_id=1, source_target_pairs={{1,0},{2,1},{3,2},{4,3},{5,4},{6,5},{7,6},{8,7},{9,8},{10,9},{11,1... | collective-permute-start | bytes 2875400 | tf_op jit(solution)/shard_map/ppermute | solution.py:21
  29.0 21.4 %collective-permute-done.1 = bf16[6,1,96,832]{3,2,1,0:T(8,128)(2,1)S(1)} collective-permute-done((bf16[6,1,96,832]{3,2,1,0:T(8,128)(2,1)S(1)}, bf16[6,1,96,832]{3,2,1,0:T(8,128)(2,1)S(1)}, u32[]{:S(2)}, u32[]{:S(2)}) %collective-permute-start.1) | collective-permute-done | bytes 958496 | tf_op jit(solution)/shard_map/ppermute | solution.py:20
  50.4 0.0 collective-permute-done.2
  50.4 0.7 maximum_bitcast_fusion
  51.2 4.8 %pad = bf16[6,4,96,1,840]{4,2,1,0,3:T(8,128)(2,1)} pad(bf16[6,4,96,1,832]{4,2,1,0,3:T(8,128)(2,1)S(1)} %maximum_bitcast_fusion, bf16[]{:T(256)} %constant.13), padding=0_0x0_0x0_0x0_0x1_7 | pad | bytes 7704578 | tf_op jit(solution)/shard_map/broadcast_in_dim | solution.py:41
  56.0 9.7 %reshape.22 = bf16[6,4,96,1,8,105]{5,4,2,1,0,3:T(8,128)(2,1)} reshape(bf16[6,4,96,1,840]{4,2,1,0,3:T(8,128)(2,1)} %pad) | data formatting | bytes 7741440 | tf_op jit(solution)/shard_map/conv_general_dilated | solution.py:40
  65.6 0.0 copy-start.7
  65.6 8.8 %copy.9 = bf16[6,4,96,1,8,105]{2,4,5,1,0,3:T(8,128)(2,1)} copy(bf16[6,4,96,1,8,105]{5,4,2,1,0,3:T(8,128)(2,1)} %reshape.22) | data formatting | bytes 7741440 | tf_op jit(solution)/shard_map/conv_general_dilated | solution.py:40
  74.4 0.9 slice.31
  75.3 0.0 copy-done
  75.3 0.0 copy-done.7
  75.4 18.4 %fusion.41 = f32[4,2,8,105,96]{4,2,3,1,0:T(8,128)} fusion(bf16[3,3,3,96,96]{4,3,2,1,0:T(8,128)(2,1)S(1)} %copy-done, bf16[6,4,96,1,7,2]{2,4,5,1,0,3:T(8,128)(2,1)S(1)} %slice.31, bf16[6,4,96,1,8,105]{2,4,5,1,0,3:T(8,128)(2,1)} %copy.9, pred[8,105]{0,1:T(8,128)(4,1)S(1)} %copy-done.7), kind=kOutput, calls=%fused_computation.51 | convolution fusion | flops 3356780544 | bytes 7014216 | tf_op jit(solution)/shard_map/conv_general_dilated | solution.py:40
  93.7 4.8 %copy.10 = f32[4,2,8,105,96]{3,2,4,1,0:T(8,128)} copy(f32[4,2,8,105,96]{4,2,3,1,0:T(8,128)} %fusion.41) | data formatting | bytes 5160960 | tf_op jit(solution)/shard_map/conv_general_dilated | solution.py:40
  98.5 0.0 copy-start.3
  98.5 3.1 %reshape.26 = f32[4,2,1,840,96]{3,4,1,0,2:T(8,128)S(1)} reshape(f32[4,2,8,105,96]{3,2,4,1,0:T(8,128)} %copy.10) | data formatting | bytes 5160960 | tf_op jit(solution)/shard_map/conv_general_dilated | solution.py:40
  101.6 0.0 copy-done.3
  101.6 0.0 copy-start.5
  101.6 0.4 fusion.16
  102.1 0.2 copy-done.5
  102.3 0.9 fusion.23
  103.2 0.1 slice.33
  103.3 1.3 collective-permute-start.3
  104.6 11.5 %collective-permute-done.3 = bf16[2,2,96,832]{3,2,1,0:T(8,128)(2,1)S(1)} collective-permute-done((bf16[2,2,96,832]{3,2,1,0:T(8,128)(2,1)S(1)}, bf16[2,2,96,832]{3,2,1,0:T(8,128)(2,1)S(1)}, u32[]{:S(2)}, u32[]{:S(2)}) %collective-permute-start.3) | collective-permute-done | bytes 639008 | tf_op jit(solution)/shard_map/ppermute | solution.py:10
  116.1 0.3 fusion.44
  116.4 1.9 collective-permute-start.4
  118.3 3.6 %collective-permute-start.5 = (bf16[6,1,96,832]{3,2,1,0:T(8,128)(2,1)S(1)}, bf16[6,1,96,832]{3,2,1,0:T(8,128)(2,1)S(1)}, u32[]{:S(2)}, u32[]{:S(2)}) collective-permute-start(bf16[6,1,96,832]{3,2,1,0:T(8,128)(2,1)S(1)} %get-tuple-element.6), channel_id=1, source_target_pairs={{1,0},{2,1},{3,2},{4,3},{5,4},{6,5},{7,6},{8,7},{9,8},{10,9},{11,1... | collective-permute-start | bytes 2875400 | tf_op jit(solution)/shard_map/ppermute | solution.py:21
  121.9 21.4 %collective-permute-done.4 = bf16[6,1,96,832]{3,2,1,0:T(8,128)(2,1)S(1)} collective-permute-done((bf16[6,1,96,832]{3,2,1,0:T(8,128)(2,1)S(1)}, bf16[6,1,96,832]{3,2,1,0:T(8,128)(2,1)S(1)}, u32[]{:S(2)}, u32[]{:S(2)}) %collective-permute-start.4) | collective-permute-done | bytes 958496 | tf_op jit(solution)/shard_map/ppermute | solution.py:20
  143.4 0.0 collective-permute-done.5
  143.4 0.7 maximum_bitcast_fusion.1
  144.1 4.8 %pad.2 = bf16[6,4,96,1,840]{4,2,1,0,3:T(8,128)(2,1)} pad(bf16[6,4,96,1,832]{4,2,1,0,3:T(8,128)(2,1)S(1)} %maximum_bitcast_fusion.1, bf16[]{:T(256)} %constant.13), padding=0_0x0_0x0_0x0_0x1_7 | pad | bytes 7704578 | tf_op jit(solution)/shard_map/broadcast_in_dim | solution.py:41
  148.9 9.7 %reshape.29 = bf16[6,4,96,1,8,105]{5,4,2,1,0,3:T(8,128)(2,1)} reshape(bf16[6,4,96,1,840]{4,2,1,0,3:T(8,128)(2,1)} %pad.2) | data formatting | bytes 7741440 | tf_op jit(solution)/shard_map/conv_general_dilated | solution.py:40
  158.5 0.0 copy-start.6
  158.5 8.8 %copy.12 = bf16[6,4,96,1,8,105]{2,4,5,1,0,3:T(8,128)(2,1)} copy(bf16[6,4,96,1,8,105]{5,4,2,1,0,3:T(8,128)(2,1)} %reshape.29) | data formatting | bytes 7741440 | tf_op jit(solution)/shard_map/conv_general_dilated | solution.py:40
  167.4 0.9 slice.36
  168.3 0.0 copy-done.6
  168.3 18.4 %fusion.38 = f32[4,2,8,105,96]{4,2,3,1,0:T(8,128)} fusion(bf16[3,3,3,96,96]{4,3,2,1,0:T(8,128)(2,1)S(1)} %copy-done.6, bf16[6,4,96,1,7,2]{2,4,5,1,0,3:T(8,128)(2,1)S(1)} %slice.36, bf16[6,4,96,1,8,105]{2,4,5,1,0,3:T(8,128)(2,1)} %copy.12, pred[8,105]{0,1:T(8,128)(4,1)S(1)} %copy-done.7), kind=kOutput, calls=%fused_computation.50 | convolution fusion | flops 3356780544 | bytes 7014216 | tf_op jit(solution)/shard_map/conv_general_dilated | solution.py:40
  186.7 4.8 %copy.13 = f32[4,2,8,105,96]{3,2,4,1,0:T(8,128)} copy(f32[4,2,8,105,96]{4,2,3,1,0:T(8,128)} %fusion.38) | data formatting | bytes 5160960 | tf_op jit(solution)/shard_map/conv_general_dilated | solution.py:40
  191.5 0.0 copy-start.2
  191.5 0.0 copy-start.4
  191.5 0.0 copy-start.1
  191.5 4.7 %reshape.33 = f32[4,2,1,840,96]{3,4,1,0,2:T(8,128)} reshape(f32[4,2,8,105,96]{3,2,4,1,0:T(8,128)} %copy.13) | data formatting | bytes 5160960 | tf_op jit(solution)/shard_map/conv_general_dilated | solution.py:40
  196.2 0.0 copy-done.2
  196.2 0.0 copy-done.4
  196.2 3.3 %fusion.32 = bf16[4,2,96,832]{3,2,1,0:T(8,128)(2,1)} fusion(bf16[4,2,96,832]{3,2,1,0:T(8,128)(2,1)S(1)} %copy-done.2, f32[4,2,1,840,96]{3,4,1,0,2:T(8,128)} %reshape.33, f32[96]{0:T(128)S(1)} %copy-done.4), kind=kLoop, calls=%fused_computation.38 | loop fusion | flops 2555904 | bytes 5112192 | tf_op jit(solution)/shard_map/convert_element_type | solution.py:60
  199.5 0.0 copy-done.1
  (2 shorter events, 0.1 us)
Async XLA Ops:
  0.0 75.3 %copy-start = (bf16[3,3,3,96,96]{4,3,2,1,0:T(8,128)(2,1)S(1)}, bf16[3,3,3,96,96]{4,3,2,1,0:T(8,128)(2,1)}, u32[]{:S(2)}) copy-start(bf16[3,3,3,96,96]{4,3,2,1,0:T(8,128)(2,1)} %param.9) | copy-start | bytes 1492996
  4.1 19.1 %collective-permute-start = (bf16[2,2,96,832]{3,2,1,0:T(8,128)(2,1)S(1)}, bf16[2,2,96,832]{3,2,1,0:T(8,128)(2,1)S(1)}, u32[]{:S(2)}, u32[]{:S(2)}) collective-permute-start(bf16[2,2,96,832]{3,2,1,0:T(8,128)(2,1)S(1)} %slice.28), channel_id=1, source_target_pairs={{0,16},{1,17},{2,18},{3,19},{4,20},{5,21},{6,22},{7,23},{8,24},{9,... | collective-permute-start | bytes 1916936 | tf_op jit(solution)/shard_map/ppermute | solution.py:10
  23.4 27.0 %collective-permute-start.1 = (bf16[6,1,96,832]{3,2,1,0:T(8,128)(2,1)S(1)}, bf16[6,1,96,832]{3,2,1,0:T(8,128)(2,1)S(1)}, u32[]{:S(2)}, u32[]{:S(2)}) collective-permute-start(bf16[6,1,96,832]{3,2,1,0:T(8,128)(2,1)S(1)} %get-tuple-element.7), channel_id=1, source_target_pairs={{0,1},{1,2},{2,3},{3,4},{4,5},{5,6},{6,7},{7,8},{8,9},{9,10},{10,1... | collective-permute-start | bytes 2875400 | tf_op jit(solution)/shard_map/ppermute | solution.py:20
  25.4 25.1 %collective-permute-start.2 = (bf16[6,1,96,832]{3,2,1,0:T(8,128)(2,1)S(1)}, bf16[6,1,96,832]{3,2,1,0:T(8,128)(2,1)S(1)}, u32[]{:S(2)}, u32[]{:S(2)}) collective-permute-start(bf16[6,1,96,832]{3,2,1,0:T(8,128)(2,1)S(1)} %get-tuple-element.8), channel_id=1, source_target_pairs={{1,0},{2,1},{3,2},{4,3},{5,4},{6,5},{7,6},{8,7},{9,8},{10,9},{11,1... | collective-permute-start | bytes 2875400 | tf_op jit(solution)/shard_map/ppermute | solution.py:21
  65.6 9.7 %copy-start.7 = (pred[8,105]{0,1:T(8,128)(4,1)S(1)}, pred[8,105]{0,1:T(8,128)(4,1)}, u32[]{:S(2)}) copy-start(pred[8,105]{0,1:T(8,128)(4,1)} %constant.21) | copy-start | bytes 2524
  98.5 3.1 %copy-start.3 = (f32[96]{0:T(128)S(1)}, f32[96]{0:T(128)}, u32[]{:S(2)}) copy-start(f32[96]{0:T(128)} %param.10) | copy-start | bytes 1156
  101.6 0.7 copy-start.5
  103.3 12.8 %collective-permute-start.3 = (bf16[2,2,96,832]{3,2,1,0:T(8,128)(2,1)S(1)}, bf16[2,2,96,832]{3,2,1,0:T(8,128)(2,1)S(1)}, u32[]{:S(2)}, u32[]{:S(2)}) collective-permute-start(bf16[2,2,96,832]{3,2,1,0:T(8,128)(2,1)S(1)} %slice.33), channel_id=1, source_target_pairs={{0,16},{1,17},{2,18},{3,19},{4,20},{5,21},{6,22},{7,23},{8,24},{9,... | collective-permute-start | bytes 1916936 | tf_op jit(solution)/shard_map/ppermute | solution.py:10
  116.4 27.0 %collective-permute-start.4 = (bf16[6,1,96,832]{3,2,1,0:T(8,128)(2,1)S(1)}, bf16[6,1,96,832]{3,2,1,0:T(8,128)(2,1)S(1)}, u32[]{:S(2)}, u32[]{:S(2)}) collective-permute-start(bf16[6,1,96,832]{3,2,1,0:T(8,128)(2,1)S(1)} %get-tuple-element.5), channel_id=1, source_target_pairs={{0,1},{1,2},{2,3},{3,4},{4,5},{5,6},{6,7},{7,8},{8,9},{9,10},{10,1... | collective-permute-start | bytes 2875400 | tf_op jit(solution)/shard_map/ppermute | solution.py:20
  118.3 25.1 %collective-permute-start.5 = (bf16[6,1,96,832]{3,2,1,0:T(8,128)(2,1)S(1)}, bf16[6,1,96,832]{3,2,1,0:T(8,128)(2,1)S(1)}, u32[]{:S(2)}, u32[]{:S(2)}) collective-permute-start(bf16[6,1,96,832]{3,2,1,0:T(8,128)(2,1)S(1)} %get-tuple-element.6), channel_id=1, source_target_pairs={{1,0},{2,1},{3,2},{4,3},{5,4},{6,5},{7,6},{8,7},{9,8},{10,9},{11,1... | collective-permute-start | bytes 2875400 | tf_op jit(solution)/shard_map/ppermute | solution.py:21
  158.5 9.8 %copy-start.6 = (bf16[3,3,3,96,96]{4,3,2,1,0:T(8,128)(2,1)S(1)}, bf16[3,3,3,96,96]{4,3,2,1,0:T(8,128)(2,1)}, u32[]{:S(2)}) copy-start(bf16[3,3,3,96,96]{4,3,2,1,0:T(8,128)(2,1)} %param.12) | copy-start | bytes 1492996
  191.5 4.7 %copy-start.2 = (bf16[4,2,96,832]{3,2,1,0:T(8,128)(2,1)S(1)}, bf16[4,2,96,832]{3,2,1,0:T(8,128)(2,1)}, u32[]{:S(2)}) copy-start(bf16[4,2,96,832]{3,2,1,0:T(8,128)(2,1)} %param.7) | copy-start | bytes 3833860
  191.5 4.7 %copy-start.4 = (f32[96]{0:T(128)S(1)}, f32[96]{0:T(128)}, u32[]{:S(2)}) copy-start(f32[96]{0:T(128)} %param.13) | copy-start | bytes 1156
  191.5 8.0 %copy-start.1 = (bf16[3,3,3,96,96]{4,3,2,1,0:T(8,128)(2,1)S(1)}, bf16[3,3,3,96,96]{4,3,2,1,0:T(8,128)(2,1)}, u32[]{:S(2)}) copy-start(bf16[3,3,3,96,96]{4,3,2,1,0:T(8,128)(2,1)} %param.9) | copy-start | bytes 1492996
where the time goes:
time: 201 us; the launch traced here: 200 us
  waiting for transfers between devices  72.2 us (36%)
  local copies, waits for them, and re-layouts  66.1 us (33%)
  matrix products  36.8 us (18%)
  starting transfers between devices  13.7 us (7%)
  other arithmetic  10.6 us (5%)
    conv_general_dilated x10, local copies, waits for them, and re-layouts, convolve(): lax.conv_general_dilated(extended[None], kernel, window_strides=(1, 1, 1)...  56.2 us
    ppermute x2, waiting for transfers between devices, padded(): before = lax.ppermute(last, axis, up)  42.8 us
    conv_general_dilated x2, matrix products, convolve(): lax.conv_general_dilated(extended[None], kernel, window_strides=(1, 1, 1)...  36.8 us
    ppermute x2, waiting for transfers between devices, shifted(): return lax.ppermute(block, axis, route)  29.3 us
    broadcast_in_dim x2, local copies, waits for them, and re-layouts, convolve(): extended[None]  9.58 us
    ppermute x2, starting transfers between devices, padded(): after = lax.ppermute(initial, axis, down)  7.28 us
  transfers between devices with their start and end apart: 6, of which 4 were waited for; matrix products, arithmetic and copies ran while one was open for 0% of the time, Pallas kernels for 0%

commit v1 on v0

v1 whole, which is shorter than its diff:
```python
import functools

import jax
import jax.numpy as jnp
from jax import lax
from jax.experimental import pallas as pl
from jax.experimental.pallas import tpu as pltpu
from jax.sharding import PartitionSpec as P


def norm_silu(values, gain):
    wide = values.astype(jnp.float32)
    mean_square = jnp.mean(wide * wide, axis=-2, keepdims=True)
    half = wide * lax.rsqrt(mean_square + 1e-06) * (0.5 * gain)
    return (half + half * jnp.tanh(half)).astype(jnp.bfloat16)


def shifted(block, axis, distance):
    devices = range(lax.axis_size(axis))
    route = [(i - distance, i) for i in devices if i - distance in devices]
    return lax.ppermute(block, axis, route)


def row_halo(block):
    return shifted(block[:, -1:], "rows", 1), shifted(block[:, :1], "rows", -1)


def act_kernel(frames, gain, out):
    for row in range(frames.shape[1]):
        out[0, row] = norm_silu(frames[0, row], gain[...])


def activate(frames, gain):
    count, rows, channels, pixels = frames.shape
    block = pl.BlockSpec((1, rows, channels, pixels), lambda i: (i, 0, 0, 0))
    return pl.pallas_call(
        act_kernel,
        grid=(count,),
        in_specs=[block, pl.BlockSpec((channels, 1), lambda i: (0, 0))],
        out_specs=block,
        out_shape=jax.ShapeDtypeStruct(frames.shape, jnp.bfloat16),
        name="activate",
    )(frames, gain)


def conv_kernel(groups, final, *refs):
    inputs, out = list(refs[:-1]), refs[-1]
    slabs = []
    for _ in range(groups):
        own, up, down = inputs[0], inputs[1], inputs[2]
        inputs = inputs[3:]
        for t in range(own.shape[0]):
            rows = [own.at[t, r] for r in range(own.shape[1])]
            slabs.append([up.at[t, 0]] + rows + [down.at[t, 0]])
    weight, bias, extra = inputs[0], inputs[1], inputs[2]
    frames, rows, channels, pixels = out.shape
    zero = jnp.zeros((channels, 1), jnp.float32)
    for t in range(frames):
        for r in range(rows):
            taps = [slabs[t + i][r + j][...] for i in range(3) for j in range(3)]
            sums = jnp.dot(
                weight[...], jnp.concatenate(taps, axis=0), preferred_element_type=jnp.float32
            )
            left = sums[:channels]
            right = sums[2 * channels :]
            result = (
                sums[channels : 2 * channels]
                + jnp.concatenate([zero, left[:, : pixels - 1]], axis=1)
                + jnp.concatenate([right[:, 1:], zero], axis=1)
                + bias[...]
            )
            if final:
                out[t, r] = (result + extra[t, r].astype(jnp.float32)).astype(jnp.bfloat16)
            else:
                out[t, r] = norm_silu(result.astype(jnp.bfloat16), extra[...])


def convolve(groups, weight, bias, extra, final, start=0, total=None, into=None, name="conv"):
    rows, channels, pixels = groups[0][0].shape[1:]
    count = sum(g[4] for g in groups) - 2
    operands, specs = [], []

    def whole(value):
        operands.append(value)
        specs.append(pl.BlockSpec(value.shape, lambda i, n=value.ndim: (0,) * n))

    for own, up, down, first, frames in groups:
        for value in (own, up, down):
            operands.append(value)
            specs.append(
                pl.BlockSpec((frames,) + value.shape[1:], lambda i, b=first // frames: (b, 0, 0, 0))
            )
    whole(weight)
    whole(bias)
    if final:
        operands.append(extra)
        specs.append(
            pl.BlockSpec((count, rows, channels, pixels), lambda i: (start // count, 0, 0, 0))
        )
    else:
        whole(extra)
    body = functools.partial(conv_kernel, len(groups), final)
    aliases = {}
    if into is not None:
        aliases = {len(operands): 0}
        operands.append(into)
        specs.append(pl.BlockSpec(memory_space=pl.ANY))
        plain = body

        def body(*refs):
            plain(*refs[:-2], refs[-1])

    return pl.pallas_call(
        body,
        grid=(1,),
        in_specs=specs,
        out_specs=pl.BlockSpec(
            (count, rows, channels, pixels), lambda i: (start // count, 0, 0, 0)
        ),
        out_shape=jax.ShapeDtypeStruct((total or count, rows, channels, pixels), jnp.bfloat16),
        input_output_aliases=aliases,
        compiler_params=pltpu.CompilerParams(vmem_limit_bytes=48 << 20),
        cost_estimate=pl.CostEstimate(
            flops=2 * 27 * channels * channels * pixels * rows * count * 2,
            bytes_accessed=8 << 20,
            transcendentals=0,
        ),
        name=name,
    )(*operands)


def on_device(
    frames_in, gain_first, kernel_first, bias_first, gain_second, kernel_second, bias_second
):
    frames, channels = frames_in.shape[0], frames_in.shape[2]
    half = frames // 2

    def matrix(kernel):
        return kernel.transpose(2, 3, 0, 1, 4).reshape(3 * channels, 9 * channels)

    first, second = matrix(kernel_first), matrix(kernel_second)
    bias_first, bias_second = bias_first[:, None], bias_second[:, None]
    gain_first, gain_second = gain_first[:, None], gain_second[:, None]

    act = activate(frames_in, gain_first)
    earlier = shifted(act[half:], "tm", 1)
    up, down = row_halo(act)
    late = convolve([(act, up, down, 0, frames)], first, bias_first, gain_second, False, name="late_first")
    earlier_up, earlier_down = row_halo(earlier)
    earlier_second = shifted(late, "tm", 1)
    late_up, late_down = row_halo(late)
    soon = convolve(
        [(earlier, earlier_up, earlier_down, 0, half), (act, up, down, 0, half)],
        first, bias_first, gain_second, False, name="soon_first",
    )
    soon_up, soon_down = row_halo(soon)
    second_up, second_down = row_halo(earlier_second)
    out = convolve(
        [(soon, soon_up, soon_down, 0, half), (late, late_up, late_down, 0, half)],
        second, bias_second, frames_in, True, half, frames, name="late_second",
    )
    return convolve(
        [(earlier_second, second_up, second_down, 0, half), (soon, soon_up, soon_down, 0, half)],
        second, bias_second, frames_in, True, 0, frames, into=out, name="soon_second",
    )


def solution(mesh):
    return jax.shard_map(
        on_device,
        mesh=mesh,
        in_specs=(P("tm", "rows", None, None), P(), P(), P(), P(), P(), P()),
        out_specs=P("tm", "rows", None, None),
        check_vma=False,
    )
```

time: 201 us -> 86.5 us (0.43)
  the two profiles are of different devices: /device:TPU:6 before, /device:TPU:3 now
where the time goes in v1:
time: 86.5 us; the launch traced here: 85.6 us
  starting transfers between devices  40 us (46%)
  local copies, waits for them, and re-layouts  21.4 us (25%)
  Pallas kernels  21 us (24%)
  waiting for transfers between devices  2.88 us (3%)
    ppermute x12, starting transfers between devices, shifted(): return lax.ppermute(block, axis, route)  40 us
    pallas_call x4, Pallas kernels, convolve(): pl.pallas_call(body, grid=(1,), in_specs=specs, out_specs=pl.BlockSpec((c...  17.1 us
    reshape x2, local copies, waits for them, and re-layouts, matrix(): return kernel.transpose(2, 3, 0, 1, 4).reshape(3 * channels, 9 * channels)  5.12 us
    unnamed x32, local copies, waits for them, and re-layouts  4.71 us
    transpose x2, local copies, waits for them, and re-layouts, matrix(): return kernel.transpose(2, 3, 0, 1, 4).reshape(3 * channels, 9 * channels)  3.94 us
    pallas_call x1, Pallas kernels, activate(): pl.pallas_call(act_kernel, grid=(count,), in_specs=[block, pl.BlockSpec((...  3.87 us
    slice x5, local copies, waits for them, and re-layouts, row_halo(): block[:, :1]  3.84 us
    ppermute x12, waiting for transfers between devices, shifted(): return lax.ppermute(block, axis, route)  2.88 us
  transfers between devices with their start and end apart: 12, of which 1 were waited for; matrix products, arithmetic and copies ran while one was open for 15% of the time, Pallas kernels for 14%

profile of v1, /device:TPU:3, one launch (start us, length us, event | category | flops | bytes accessed | tf_op | source)
XLA Modules:
  0.0 85.6 jit_solution(8772255830347102183)
XLA Ops:
  0.0 1.4 %copy.18.gain = f32[96,1]{1,0:T(8,128)} copy(f32[96,1]{0,1:T(1,128)} %bitcast.8) | data formatting | bytes 768 | tf_op jit(solution)/shard_map/broadcast_in_dim | solution.py:143
  1.4 3.9 %activate.1.refs_0_.refs_3_ = bf16[4,2,96,832]{3,2,1,0:T(8,128)(2,1)} custom-call(bf16[4,2,96,832]{3,2,1,0:T(8,128)(2,1)} %refs_8_.3, f32[96,1]{1,0:T(8,128)} %copy.18.gain), custom_call_target="tpu_custom_call" | custom-call | tf_op jit(solution)/shard_map/activate/pallas_call | solution.py:36
  5.2 2.1 %slice.48 = bf16[2,2,96,832]{3,2,1,0:T(8,128)(2,1)} slice(bf16[4,2,96,832]{3,2,1,0:T(8,128)(2,1)} %activate.1.refs_0_.refs_3_), slice={[2:4], [0:2], [0:96], [0:832]} | slice | bytes 1277952 | tf_op jit(solution)/shard_map/slice | solution.py:146
  7.4 3.3 %collective-permute-start.5 = (bf16[2,2,96,832]{3,2,1,0:T(8,128)(2,1)}, bf16[2,2,96,832]{3,2,1,0:T(8,128)(2,1)S(1)}, u32[]{:S(2)}, u32[]{:S(2)}) collective-permute-start(bf16[2,2,96,832]{3,2,1,0:T(8,128)(2,1)} %slice.48), channel_id=1, source_target_pairs={{0,16},{1,17},{2,18},{3,19},{4,20},{5,21},{6,22},{7,23},{8,24},{9,... | collective-permute-start | bytes 1916936 | tf_op jit(solution)/shard_map/ppermute | solution.py:21
  10.7 0.0 copy-done
  10.7 1.2 %fusion = (bf16[4,1,96,832]{3,2,1,0:T(8,128)(2,1)}, bf16[4,1,96,832]{3,2,1,0:T(8,128)(2,1)}) fusion(bf16[4,2,96,832]{3,2,1,0:T(8,128)(2,1)S(1)} %copy-done), kind=kLoop, calls=%fused_computation | loop fusion | bytes 2555904 | tf_op jit(solution)/shard_map/slice | solution.py:25
  11.9 2.9 %collective-permute-start.1 = (bf16[4,1,96,832]{3,2,1,0:T(8,128)(2,1)}, bf16[4,1,96,832]{3,2,1,0:T(8,128)(2,1)S(1)}, u32[]{:S(2)}, u32[]{:S(2)}) collective-permute-start(bf16[4,1,96,832]{3,2,1,0:T(8,128)(2,1)} %get-tuple-element.5), channel_id=1, source_target_pairs={{1,0},{2,1},{3,2},{4,3},{5,4},{6,5},{7,6},{8,7},{9,8},{10,9},{11,1... | collective-permute-start | bytes 1916936 | tf_op jit(solution)/shard_map/ppermute | solution.py:21
  14.7 3.6 %collective-permute-start = (bf16[4,1,96,832]{3,2,1,0:T(8,128)(2,1)}, bf16[4,1,96,832]{3,2,1,0:T(8,128)(2,1)}, u32[]{:S(2)}, u32[]{:S(2)}) collective-permute-start(bf16[4,1,96,832]{3,2,1,0:T(8,128)(2,1)} %get-tuple-element.6), channel_id=1, source_target_pairs={{0,1},{1,2},{2,3},{3,4},{4,5},{5,6},{6,7},{7,8},{8,9},{9,10},{10,1... | collective-permute-start | bytes 1916936 | tf_op jit(solution)/shard_map/ppermute | solution.py:21
  18.3 0.0 copy-done.13
  18.4 0.1 copy.20.refs_4_.refs_7_
  18.5 0.0 copy-done.14
  18.5 0.1 copy.21.refs_5_.refs_8_
  18.6 0.0 copy-done.12
  18.6 1.4 %copy.19 = bf16[3,96,3,3,96]{4,3,2,1,0:T(4,128)(2,1)} copy(bf16[3,96,3,3,96]{4,1,0,3,2:T(8,128)(2,1)S(1)} %bitcast.6) | data formatting | bytes 995328 | tf_op jit(solution)/shard_map/transpose | solution.py:139
  19.9 2.2 %reshape.6.refs_3_.refs_6_ = bf16[288,864]{1,0:T(8,128)(2,1)S(1)} reshape(bf16[3,96,3,3,96]{4,3,2,1,0:T(4,128)(2,1)} %copy.19) | data formatting | bytes 995328 | tf_op jit(solution)/shard_map/reshape | solution.py:139
  22.2 0.0 copy-start.4
  22.2 2.9 %collective-permute-done.5.refs_0_ = bf16[2,2,96,832]{3,2,1,0:T(8,128)(2,1)S(1)} collective-permute-done((bf16[2,2,96,832]{3,2,1,0:T(8,128)(2,1)}, bf16[2,2,96,832]{3,2,1,0:T(8,128)(2,1)S(1)}, u32[]{:S(2)}, u32[]{:S(2)}) %collective-permute-start.5) | collective-permute-done | bytes 639008 | tf_op jit(solution)/shard_map/ppermute | solution.py:21
  25.0 0.1 fusion.3
  25.1 3.4 %collective-permute-start.7 = (bf16[2,1,96,832]{3,2,1,0:T(8,128)(2,1)S(1)}, bf16[2,1,96,832]{3,2,1,0:T(8,128)(2,1)S(1)}, u32[]{:S(2)}, u32[]{:S(2)}) collective-permute-start(bf16[2,1,96,832]{3,2,1,0:T(8,128)(2,1)S(1)} %get-tuple-element.11), channel_id=1, source_target_pairs={{1,0},{2,1},{3,2},{4,3},{5,4},{6,5},{7,6},{8,7},{9,8},{10,9},{11,1... | collective-permute-start | bytes 958472 | tf_op jit(solution)/shard_map/ppermute | solution.py:21
  28.6 3.1 %collective-permute-start.6 = (bf16[2,1,96,832]{3,2,1,0:T(8,128)(2,1)S(1)}, bf16[2,1,96,832]{3,2,1,0:T(8,128)(2,1)S(1)}, u32[]{:S(2)}, u32[]{:S(2)}) collective-permute-start(bf16[2,1,96,832]{3,2,1,0:T(8,128)(2,1)S(1)} %get-tuple-element.12), channel_id=1, source_target_pairs={{0,1},{1,2},{2,3},{3,4},{4,5},{5,6},{6,7},{7,8},{8,9},{9,10},{10,1... | collective-permute-start | bytes 958472 | tf_op jit(solution)/shard_map/ppermute | solution.py:21
  31.6 0.0 collective-permute-done.1.refs_2_.refs_5_
  31.6 0.0 copy-start.7
  31.7 0.8 copy-done.7
  32.5 0.0 collective-permute-done.refs_1_.refs_4_
  32.5 0.0 copy-done.2
  32.5 1.1 %copy-done.8 = bf16[4,1,96,832]{3,2,1,0:T(8,128)(2,1)S(1)} copy-done((bf16[4,1,96,832]{3,2,1,0:T(8,128)(2,1)S(1)}, bf16[4,1,96,832]{3,2,1,0:T(8,128)(2,1)}, u32[]{:S(2)}) %copy-start.8) | copy-done | bytes 639000
  33.6 3.9 %late_first.1.refs_3_ = bf16[2,2,96,832]{3,2,1,0:T(8,128)(2,1)S(1)} custom-call(bf16[4,2,96,832]{3,2,1,0:T(8,128)(2,1)S(1)} %copy-done, bf16[4,1,96,832]{3,2,1,0:T(8,128)(2,1)} %collective-permute-done.refs_1_.refs_4_, bf16[4,1,96,832]{3,2,1,0:T(8,128)(2,1)S(1)} %copy-done.8, bf16[288,864]{1,0:T(8,128)(2,1)S(1)} %reshape.6.refs_3_.refs_6_, ...), custom_call_target="tpu_custom_call" | custom-call | flops 3312451584 | bytes 8388608 | tf_op jit(solution)/shard_map/late_first/pallas_call | solution.py:113
  37.5 0.0 copy-done.4
  37.5 0.0 copy-start.3
  37.5 4.2 %collective-permute-start.2 = (bf16[2,2,96,832]{3,2,1,0:T(8,128)(2,1)S(1)}, bf16[2,2,96,832]{3,2,1,0:T(8,128)(2,1)S(1)}, u32[]{:S(2)}, u32[]{:S(2)}) collective-permute-start(bf16[2,2,96,832]{3,2,1,0:T(8,128)(2,1)S(1)} %late_first.1.refs_3_), channel_id=1, source_target_pairs={{0,16},{1,17},{2,18},{3,19},{4,20},{5,21},{6,22},{7,23},{8,24},{9,... | collective-permute-start | bytes 1916936 | tf_op jit(solution)/shard_map/ppermute | solution.py:21
  41.8 0.0 copy-start.5
  41.8 0.8 fusion.1
  42.5 3.7 %collective-permute-start.11 = (bf16[2,1,96,832]{3,2,1,0:T(8,128)(2,1)S(1)}, bf16[2,1,96,832]{3,2,1,0:T(8,128)(2,1)S(1)}, u32[]{:S(2)}, u32[]{:S(2)}) collective-permute-start(bf16[2,1,96,832]{3,2,1,0:T(8,128)(2,1)S(1)} %get-tuple-element.7), channel_id=1, source_target_pairs={{1,0},{2,1},{3,2},{4,3},{5,4},{6,5},{7,6},{8,7},{9,8},{10,9},{11,1... | collective-permute-start | bytes 958472 | tf_op jit(solution)/shard_map/ppermute | solution.py:21
  46.3 2.7 %collective-permute-start.10 = (bf16[2,1,96,832]{3,2,1,0:T(8,128)(2,1)}, bf16[2,1,96,832]{3,2,1,0:T(8,128)(2,1)}, u32[]{:S(2)}, u32[]{:S(2)}) collective-permute-start(bf16[2,1,96,832]{3,2,1,0:T(8,128)(2,1)} %get-tuple-element.8), channel_id=1, source_target_pairs={{0,1},{1,2},{2,3},{3,4},{4,5},{5,6},{6,7},{7,8},{8,9},{9,10},{10,1... | collective-permute-start | bytes 958472 | tf_op jit(solution)/shard_map/ppermute | solution.py:21
  49.0 0.0 collective-permute-done.7.refs_2_
  49.0 0.0 collective-permute-done.6.refs_1_
  49.0 0.0 copy-done.9
  49.0 0.0 copy-done.3
  49.1 0.0 copy-done.5
  49.1 3.7 %soon_first.1.refs_0_.refs_3_ = bf16[2,2,96,832]{3,2,1,0:T(8,128)(2,1)S(1)} custom-call(bf16[2,2,96,832]{3,2,1,0:T(8,128)(2,1)S(1)} %copy-done.3, bf16[2,1,96,832]{3,2,1,0:T(8,128)(2,1)S(1)} %collective-permute-done.6.refs_1_, bf16[2,1,96,832]{3,2,1,0:T(8,128)(2,1)S(1)} %collective-permute-done.7.refs_2_, bf16[4,2,96,832]{3,2,1,0:T(8,128)(2,1)S(1)} %copy-done, ...), custom_call_target="tpu_custom_call" | custom-call | flops 3312451584 | bytes 8388608 | tf_op jit(solution)/shard_map/soon_first/pallas_call | solution.py:113
  52.8 0.0 copy-start.15
  52.8 0.9 %fusion.2 = (bf16[2,1,96,832]{3,2,1,0:T(8,128)(2,1)}, bf16[2,1,96,832]{3,2,1,0:T(8,128)(2,1)}) fusion(bf16[2,2,96,832]{3,2,1,0:T(8,128)(2,1)S(1)} %soon_first.1.refs_0_.refs_3_), kind=kLoop, calls=%fused_computation.2 | loop fusion | bytes 1277952 | tf_op jit(solution)/shard_map/slice | solution.py:25
  53.7 1.9 %collective-permute-start.9 = (bf16[2,1,96,832]{3,2,1,0:T(8,128)(2,1)}, bf16[2,1,96,832]{3,2,1,0:T(8,128)(2,1)}, u32[]{:S(2)}, u32[]{:S(2)}) collective-permute-start(bf16[2,1,96,832]{3,2,1,0:T(8,128)(2,1)} %get-tuple-element.9), channel_id=1, source_target_pairs={{1,0},{2,1},{3,2},{4,3},{5,4},{6,5},{7,6},{8,7},{9,8},{10,9},{11,1... | collective-permute-start | bytes 958472 | tf_op jit(solution)/shard_map/ppermute | solution.py:21
  55.6 4.5 %collective-permute-start.8 = (bf16[2,1,96,832]{3,2,1,0:T(8,128)(2,1)}, bf16[2,1,96,832]{3,2,1,0:T(8,128)(2,1)}, u32[]{:S(2)}, u32[]{:S(2)}) collective-permute-start(bf16[2,1,96,832]{3,2,1,0:T(8,128)(2,1)} %get-tuple-element.10), channel_id=1, source_target_pairs={{0,1},{1,2},{2,3},{3,4},{4,5},{5,6},{6,7},{7,8},{8,9},{9,10},{10,1... | collective-permute-start | bytes 958472 | tf_op jit(solution)/shard_map/ppermute | solution.py:21
  60.2 0.0 collective-permute-done.2.refs_0_
  60.2 0.9 %fusion.4 = (bf16[2,1,96,832]{3,2,1,0:T(8,128)(2,1)}, bf16[2,1,96,832]{3,2,1,0:T(8,128)(2,1)}) fusion(bf16[2,2,96,832]{3,2,1,0:T(8,128)(2,1)S(1)} %collective-permute-done.2.refs_0_), kind=kLoop, calls=%fused_computation.4 | loop fusion | bytes 1277952 | tf_op jit(solution)/shard_map/slice | solution.py:25
  61.1 1.9 %collective-permute-start.4 = (bf16[2,1,96,832]{3,2,1,0:T(8,128)(2,1)}, bf16[2,1,96,832]{3,2,1,0:T(8,128)(2,1)}, u32[]{:S(2)}, u32[]{:S(2)}) collective-permute-start(bf16[2,1,96,832]{3,2,1,0:T(8,128)(2,1)} %get-tuple-element.13), channel_id=1, source_target_pairs={{1,0},{2,1},{3,2},{4,3},{5,4},{6,5},{7,6},{8,7},{9,8},{10,9},{11,1... | collective-permute-start | bytes 958472 | tf_op jit(solution)/shard_map/ppermute | solution.py:21
  63.0 0.0 collective-permute-done.11.refs_5_
  63.0 0.7 copy-done.10
  63.7 4.7 %collective-permute-start.3 = (bf16[2,1,96,832]{3,2,1,0:T(8,128)(2,1)}, bf16[2,1,96,832]{3,2,1,0:T(8,128)(2,1)}, u32[]{:S(2)}, u32[]{:S(2)}) collective-permute-start(bf16[2,1,96,832]{3,2,1,0:T(8,128)(2,1)} %get-tuple-element.14), channel_id=1, source_target_pairs={{0,1},{1,2},{2,3},{3,4},{4,5},{5,6},{6,7},{7,8},{8,9},{9,10},{10,1... | collective-permute-start | bytes 958472 | tf_op jit(solution)/shard_map/ppermute | solution.py:21
  68.5 0.1 copy.26.refs_7_
  68.6 2.6 %copy.24 = bf16[3,96,3,3,96]{4,3,2,1,0:T(4,128)(2,1)} copy(bf16[3,96,3,3,96]{4,1,0,3,2:T(8,128)(2,1)} %bitcast.7) | data formatting | bytes 995328 | tf_op jit(solution)/shard_map/transpose | solution.py:139
  71.1 2.9 %reshape.7.refs_6_ = bf16[288,864]{1,0:T(8,128)(2,1)} reshape(bf16[3,96,3,3,96]{4,3,2,1,0:T(4,128)(2,1)} %copy.24) | data formatting | bytes 995328 | tf_op jit(solution)/shard_map/reshape | solution.py:139
  74.0 0.0 collective-permute-done.10.refs_4_
  74.0 0.0 collective-permute-done.9.refs_2_.refs_5_
  74.0 0.0 collective-permute-done.8.refs_1_.refs_4_
  74.0 0.0 copy-done.1
  74.0 0.0 copy-start.6
  74.1 1.0 %copy-done.6 = bf16[288,864]{1,0:T(8,128)(2,1)S(1)} copy-done((bf16[288,864]{1,0:T(8,128)(2,1)S(1)}, bf16[288,864]{1,0:T(8,128)(2,1)}, u32[]{:S(2)}) %copy-start.6) | copy-done | bytes 497688
  75.1 1.0 %copy-done.11 = bf16[2,1,96,832]{3,2,1,0:T(8,128)(2,1)S(1)} copy-done((bf16[2,1,96,832]{3,2,1,0:T(8,128)(2,1)S(1)}, bf16[2,1,96,832]{3,2,1,0:T(8,128)(2,1)}, u32[]{:S(2)}) %copy-start.11) | copy-done | bytes 319512
  76.1 4.7 %late_second.1.refs_9_ = bf16[4,2,96,832]{3,2,1,0:T(8,128)(2,1)} custom-call(bf16[2,2,96,832]{3,2,1,0:T(8,128)(2,1)S(1)} %soon_first.1.refs_0_.refs_3_, bf16[2,1,96,832]{3,2,1,0:T(8,128)(2,1)} %collective-permute-done.8.refs_1_.refs_4_, bf16[2,1,96,832]{3,2,1,0:T(8,128)(2,1)} %collective-permute-done.9.refs_2_.refs_5_, ...), custom_call_target="tpu_custom_call" | custom-call | flops 3312451584 | bytes 8388608 | tf_op jit(solution)/shard_map/late_second/pallas_call | solution.py:113
  80.8 0.0 collective-permute-done.4.refs_2_
  80.8 0.0 collective-permute-done.3.refs_1_
  80.8 4.8 %soon_second.1 = bf16[4,2,96,832]{3,2,1,0:T(8,128)(2,1)} custom-call(bf16[2,2,96,832]{3,2,1,0:T(8,128)(2,1)S(1)} %collective-permute-done.2.refs_0_, bf16[2,1,96,832]{3,2,1,0:T(8,128)(2,1)} %collective-permute-done.3.refs_1_, bf16[2,1,96,832]{3,2,1,0:T(8,128)(2,1)} %collective-permute-done.4.refs_2_, ...), custom_call_target="tpu_custom_call", output_to_operand_aliasing={{}: (9, {})} | custom-call | flops 3312451584 | bytes 8388608 | tf_op jit(solution)/shard_map/soon_second/pallas_call | solution.py:113
  (11 shorter events, 0.0 us)
Async XLA Ops:
  5.2 5.4 %copy-start = (bf16[4,2,96,832]{3,2,1,0:T(8,128)(2,1)S(1)}, bf16[4,2,96,832]{3,2,1,0:T(8,128)(2,1)}, u32[]{:S(2)}) copy-start(bf16[4,2,96,832]{3,2,1,0:T(8,128)(2,1)} %activate.1.refs_0_.refs_3_) | copy-start | bytes 3833860
  7.4 11.0 %copy-start.13 = (f32[96]{0:T(128)S(1)}, f32[96]{0:T(128)}, u32[]{:S(2)}) copy-start(f32[96]{0:T(128)} %param.10) | copy-start | bytes 1156
  7.4 11.1 %copy-start.14 = (f32[96]{0:T(128)S(1)}, f32[96]{0:T(128)}, u32[]{:S(2)}) copy-start(f32[96]{0:T(128)} %param.11) | copy-start | bytes 1156
  7.4 11.2 %copy-start.12 = (bf16[3,3,3,96,96]{4,3,2,1,0:T(8,128)(2,1)S(1)}, bf16[3,3,3,96,96]{4,3,2,1,0:T(8,128)(2,1)}, u32[]{:S(2)}) copy-start(bf16[3,3,3,96,96]{4,3,2,1,0:T(8,128)(2,1)} %param.9) | copy-start | bytes 1492996
  7.4 17.7 %collective-permute-start.5 = (bf16[2,2,96,832]{3,2,1,0:T(8,128)(2,1)}, bf16[2,2,96,832]{3,2,1,0:T(8,128)(2,1)S(1)}, u32[]{:S(2)}, u32[]{:S(2)}) collective-permute-start(bf16[2,2,96,832]{3,2,1,0:T(8,128)(2,1)} %slice.48), channel_id=1, source_target_pairs={{0,16},{1,17},{2,18},{3,19},{4,20},{5,21},{6,22},{7,23},{8,24},{9,... | collective-permute-start | bytes 1916936 | tf_op jit(solution)/shard_map/ppermute | solution.py:21
  11.9 19.8 %collective-permute-start.1 = (bf16[4,1,96,832]{3,2,1,0:T(8,128)(2,1)}, bf16[4,1,96,832]{3,2,1,0:T(8,128)(2,1)S(1)}, u32[]{:S(2)}, u32[]{:S(2)}) collective-permute-start(bf16[4,1,96,832]{3,2,1,0:T(8,128)(2,1)} %get-tuple-element.5), channel_id=1, source_target_pairs={{1,0},{2,1},{3,2},{4,3},{5,4},{6,5},{7,6},{8,7},{9,8},{10,9},{11,1... | collective-permute-start | bytes 1916936 | tf_op jit(solution)/shard_map/ppermute | solution.py:21
  14.7 17.8 %collective-permute-start = (bf16[4,1,96,832]{3,2,1,0:T(8,128)(2,1)}, bf16[4,1,96,832]{3,2,1,0:T(8,128)(2,1)}, u32[]{:S(2)}, u32[]{:S(2)}) collective-permute-start(bf16[4,1,96,832]{3,2,1,0:T(8,128)(2,1)} %get-tuple-element.6), channel_id=1, source_target_pairs={{0,1},{1,2},{2,3},{3,4},{4,5},{5,6},{6,7},{7,8},{8,9},{9,10},{10,1... | collective-permute-start | bytes 1916936 | tf_op jit(solution)/shard_map/ppermute | solution.py:21
  22.2 15.3 %copy-start.4 = (bf16[288,864]{1,0:T(8,128)(2,1)}, bf16[288,864]{1,0:T(8,128)(2,1)S(1)}, u32[]{:S(2)}) copy-start(bf16[288,864]{1,0:T(8,128)(2,1)S(1)} %reshape.6.refs_3_.refs_6_) | copy-start | bytes 1492996
  25.0 7.5 %copy-start.2 = (bf16[2,2,96,832]{3,2,1,0:T(8,128)(2,1)}, bf16[2,2,96,832]{3,2,1,0:T(8,128)(2,1)S(1)}, u32[]{:S(2)}) copy-start(bf16[2,2,96,832]{3,2,1,0:T(8,128)(2,1)S(1)} %collective-permute-done.5.refs_0_) | copy-start | bytes 1916932
  25.1 23.9 %collective-permute-start.7 = (bf16[2,1,96,832]{3,2,1,0:T(8,128)(2,1)S(1)}, bf16[2,1,96,832]{3,2,1,0:T(8,128)(2,1)S(1)}, u32[]{:S(2)}, u32[]{:S(2)}) collective-permute-start(bf16[2,1,96,832]{3,2,1,0:T(8,128)(2,1)S(1)} %get-tuple-element.11), channel_id=1, source_target_pairs={{1,0},{2,1},{3,2},{4,3},{5,4},{6,5},{7,6},{8,7},{9,8},{10,9},{11,1... | collective-permute-start | bytes 958472 | tf_op jit(solution)/shard_map/ppermute | solution.py:21
  28.6 20.5 %collective-permute-start.6 = (bf16[2,1,96,832]{3,2,1,0:T(8,128)(2,1)S(1)}, bf16[2,1,96,832]{3,2,1,0:T(8,128)(2,1)S(1)}, u32[]{:S(2)}, u32[]{:S(2)}) collective-permute-start(bf16[2,1,96,832]{3,2,1,0:T(8,128)(2,1)S(1)} %get-tuple-element.12), channel_id=1, source_target_pairs={{0,1},{1,2},{2,3},{3,4},{4,5},{5,6},{6,7},{7,8},{8,9},{9,10},{10,1... | collective-permute-start | bytes 958472 | tf_op jit(solution)/shard_map/ppermute | solution.py:21
  31.6 0.8 copy-start.7
  32.5 1.1 %copy-start.8 = (bf16[4,1,96,832]{3,2,1,0:T(8,128)(2,1)S(1)}, bf16[4,1,96,832]{3,2,1,0:T(8,128)(2,1)}, u32[]{:S(2)}) copy-start(bf16[4,1,96,832]{3,2,1,0:T(8,128)(2,1)} %copy-done.7) | copy-start | bytes 1916932
  33.6 15.4 %copy-start.9 = (bf16[4,1,96,832]{3,2,1,0:T(8,128)(2,1)S(1)}, bf16[4,1,96,832]{3,2,1,0:T(8,128)(2,1)}, u32[]{:S(2)}) copy-start(bf16[4,1,96,832]{3,2,1,0:T(8,128)(2,1)} %copy-done.7) | copy-start | bytes 1916932
  37.5 11.5 %copy-start.3 = (bf16[2,2,96,832]{3,2,1,0:T(8,128)(2,1)S(1)}, bf16[2,2,96,832]{3,2,1,0:T(8,128)(2,1)}, u32[]{:S(2)}) copy-start(bf16[2,2,96,832]{3,2,1,0:T(8,128)(2,1)} %copy-done.2) | copy-start | bytes 1916932
  37.5 22.6 %collective-permute-start.2 = (bf16[2,2,96,832]{3,2,1,0:T(8,128)(2,1)S(1)}, bf16[2,2,96,832]{3,2,1,0:T(8,128)(2,1)S(1)}, u32[]{:S(2)}, u32[]{:S(2)}) collective-permute-start(bf16[2,2,96,832]{3,2,1,0:T(8,128)(2,1)S(1)} %late_first.1.refs_3_), channel_id=1, source_target_pairs={{0,16},{1,17},{2,18},{3,19},{4,20},{5,21},{6,22},{7,23},{8,24},{9,... | collective-permute-start | bytes 1916936 | tf_op jit(solution)/shard_map/ppermute | solution.py:21
  41.8 7.3 %copy-start.5 = (bf16[288,864]{1,0:T(8,128)(2,1)S(1)}, bf16[288,864]{1,0:T(8,128)(2,1)}, u32[]{:S(2)}) copy-start(bf16[288,864]{1,0:T(8,128)(2,1)} %copy-done.4) | copy-start | bytes 1492996
  42.5 20.4 %collective-permute-start.11 = (bf16[2,1,96,832]{3,2,1,0:T(8,128)(2,1)S(1)}, bf16[2,1,96,832]{3,2,1,0:T(8,128)(2,1)S(1)}, u32[]{:S(2)}, u32[]{:S(2)}) collective-permute-start(bf16[2,1,96,832]{3,2,1,0:T(8,128)(2,1)S(1)} %get-tuple-element.7), channel_id=1, source_target_pairs={{1,0},{2,1},{3,2},{4,3},{5,4},{6,5},{7,6},{8,7},{9,8},{10,9},{11,1... | collective-permute-start | bytes 958472 | tf_op jit(solution)/shard_map/ppermute | solution.py:21
  46.3 27.8 %collective-permute-start.10 = (bf16[2,1,96,832]{3,2,1,0:T(8,128)(2,1)}, bf16[2,1,96,832]{3,2,1,0:T(8,128)(2,1)}, u32[]{:S(2)}, u32[]{:S(2)}) collective-permute-start(bf16[2,1,96,832]{3,2,1,0:T(8,128)(2,1)} %get-tuple-element.8), channel_id=1, source_target_pairs={{0,1},{1,2},{2,3},{3,4},{4,5},{5,6},{6,7},{7,8},{8,9},{9,10},{10,1... | collective-permute-start | bytes 958472 | tf_op jit(solution)/shard_map/ppermute | solution.py:21
  52.8 15.7 %copy-start.15 = (f32[96]{0:T(128)S(1)}, f32[96]{0:T(128)}, u32[]{:S(2)}) copy-start(f32[96]{0:T(128)} %param.13) | copy-start | bytes 1156
  53.7 20.3 %collective-permute-start.9 = (bf16[2,1,96,832]{3,2,1,0:T(8,128)(2,1)}, bf16[2,1,96,832]{3,2,1,0:T(8,128)(2,1)}, u32[]{:S(2)}, u32[]{:S(2)}) collective-permute-start(bf16[2,1,96,832]{3,2,1,0:T(8,128)(2,1)} %get-tuple-element.9), channel_id=1, source_target_pairs={{1,0},{2,1},{3,2},{4,3},{5,4},{6,5},{7,6},{8,7},{9,8},{10,9},{11,1... | collective-permute-start | bytes 958472 | tf_op jit(solution)/shard_map/ppermute | solution.py:21
  55.6 18.4 %collective-permute-start.8 = (bf16[2,1,96,832]{3,2,1,0:T(8,128)(2,1)}, bf16[2,1,96,832]{3,2,1,0:T(8,128)(2,1)}, u32[]{:S(2)}, u32[]{:S(2)}) collective-permute-start(bf16[2,1,96,832]{3,2,1,0:T(8,128)(2,1)} %get-tuple-element.10), channel_id=1, source_target_pairs={{0,1},{1,2},{2,3},{3,4},{4,5},{5,6},{6,7},{7,8},{8,9},{9,10},{10,1... | collective-permute-start | bytes 958472 | tf_op jit(solution)/shard_map/ppermute | solution.py:21
  61.1 19.7 %collective-permute-start.4 = (bf16[2,1,96,832]{3,2,1,0:T(8,128)(2,1)}, bf16[2,1,96,832]{3,2,1,0:T(8,128)(2,1)}, u32[]{:S(2)}, u32[]{:S(2)}) collective-permute-start(bf16[2,1,96,832]{3,2,1,0:T(8,128)(2,1)} %get-tuple-element.13), channel_id=1, source_target_pairs={{1,0},{2,1},{3,2},{4,3},{5,4},{6,5},{7,6},{8,7},{9,8},{10,9},{11,1... | collective-permute-start | bytes 958472 | tf_op jit(solution)/shard_map/ppermute | solution.py:21
  63.0 0.7 copy-start.10
  63.7 17.1 %collective-permute-start.3 = (bf16[2,1,96,832]{3,2,1,0:T(8,128)(2,1)}, bf16[2,1,96,832]{3,2,1,0:T(8,128)(2,1)}, u32[]{:S(2)}, u32[]{:S(2)}) collective-permute-start(bf16[2,1,96,832]{3,2,1,0:T(8,128)(2,1)} %get-tuple-element.14), channel_id=1, source_target_pairs={{0,1},{1,2},{2,3},{3,4},{4,5},{5,6},{6,7},{7,8},{8,9},{9,10},{10,1... | collective-permute-start | bytes 958472 | tf_op jit(solution)/shard_map/ppermute | solution.py:21
  68.6 5.5 %copy-start.1 = (bf16[4,2,96,832]{3,2,1,0:T(8,128)(2,1)S(1)}, bf16[4,2,96,832]{3,2,1,0:T(8,128)(2,1)}, u32[]{:S(2)}) copy-start(bf16[4,2,96,832]{3,2,1,0:T(8,128)(2,1)} %refs_8_.3) | copy-start | bytes 3833860
  74.0 1.0 %copy-start.6 = (bf16[288,864]{1,0:T(8,128)(2,1)S(1)}, bf16[288,864]{1,0:T(8,128)(2,1)}, u32[]{:S(2)}) copy-start(bf16[288,864]{1,0:T(8,128)(2,1)} %reshape.7.refs_6_) | copy-start | bytes 1492996
  75.1 1.0 %copy-start.11 = (bf16[2,1,96,832]{3,2,1,0:T(8,128)(2,1)S(1)}, bf16[2,1,96,832]{3,2,1,0:T(8,128)(2,1)}, u32[]{:S(2)}) copy-start(bf16[2,1,96,832]{3,2,1,0:T(8,128)(2,1)} %copy-done.10) | copy-start | bytes 958468
